TPU v7x, 32 devices: a whole 2x2x4 slice. The times are simulated.
32 devices in a mesh: dp: 2 (over y), seq: 16 (over z, x, core).
Axes of the slice: x: 2, y: 2, z: 4, core: 2. Of those that a mesh axis runs over, the one named last changes fastest.
Arguments:
- tokens: bfloat16 [2, 4096, 768], P('dp', 'seq'), may hold values from -6 to 6
- segment_ids: int32 [2, 4096], P('dp', 'seq'), may hold values from 0 to 7, never falling along the last dimension, each value on 1 to 2048 neighbouring positions
- features: bfloat16 [12, 64, 256], replicated, may hold values from -6 to 6
- query_weight: bfloat16 [768, 768], replicated, may hold values from -0.15625 to 0.15625
- key_weight: bfloat16 [768, 768], replicated, may hold values from -0.15625 to 0.15625
- value_weight: bfloat16 [768, 768], replicated, may hold values from -0.21875 to 0.21875
- out_weight: bfloat16 [768, 768], replicated, may hold values from -0.875 to 0.875
- up_weight: bfloat16 [768, 3072], replicated, may hold values from -0.21875 to 0.21875
- down_weight: bfloat16 [3072, 768], replicated, may hold values from -0.109375 to 0.109375
- first_gain: float32 [768], replicated, may hold values from 0.1 to 1.9
- first_bias: float32 [768], replicated, may hold values from -3 to 3
- second_gain: float32 [768], replicated, may hold values from 0.1 to 1.9
- second_bias: float32 [768], replicated, may hold values from -3 to 3
- cotangent: bfloat16 [2, 4096, 768], P('dp', 'seq'), may hold values from -6 to 6
Outputs:
- output: bfloat16 [2, 4096, 768], P('dp', 'seq')
- grad_tokens: bfloat16 [2, 4096, 768], P('dp', 'seq')
- grad_query: float32 [768, 768], replicated
- grad_key: float32 [768, 768], replicated
- grad_value: float32 [768, 768], replicated
- grad_out: float32 [768, 768], replicated
- grad_up: float32 [768, 3072], replicated
- grad_down: float32 [3072, 768], replicated
- grad_first_gain: float32 [768], replicated
- grad_first_bias: float32 [768], replicated
- grad_second_gain: float32 [768], replicated
- grad_second_bias: float32 [768], replicated
Inputs may be any that keep to these rules, and one draw needn't show every extreme that they name: `segment_ids`: in each row the ids never fall, every id from 0 to 7 occurs, each on 1 to 2048 positions, and one on exactly 2048.
All inputs are finite; a program needn't handle non-finite values.
Results may differ from a plain program's by a relative error of at most 0.02.
Values sent between devices are 32-bit elements; how exact they have to be, the bound alone decides.
No kernel may reach another device: no remote copies, remote signals or barrier semaphores. Data moves between devices by JAX's collectives and lax.ppermute only.
A program may use at most 320 MiB of HBM per device.

v0:
```python
from functools import partial
import jax
import jax.numpy as jnp
from jax import lax
from jax.sharding import PartitionSpec as P

SEGS = 8
EPSILON = 1e-06
HIGHEST = lax.Precision.HIGHEST


def carried_in(value, axis, combine, identity, reverse):
    length, place = (lax.axis_size(axis), lax.axis_index(axis))
    everything = jax.tree.map(lambda part: lax.all_gather(part, axis), value)
    start = jax.tree.map(
        lambda part, zero: jnp.broadcast_to(jnp.asarray(zero, part.dtype), part.shape),
        value,
        identity,
    )

    def hop(k, before):
        at = length - 1 - k if reverse else k
        reached = at > place if reverse else at < place
        new = combine(before, jax.tree.map(lambda part: part[at], everything))
        return jax.tree.map(lambda a, b: jnp.where(reached, a, b), new, before)

    return lax.fori_loop(0, length, hop, start)


def norm_forward(hidden, norm_gain, norm_bias):
    row_mean = jnp.mean(hidden, -1, keepdims=True)
    centered = hidden - row_mean
    variance = jnp.mean(centered * centered, -1, keepdims=True)
    inv_std = lax.rsqrt(variance + EPSILON)
    normed = centered * inv_std
    return (normed * norm_gain + norm_bias, normed, inv_std)


def norm_backward(upstream, normed, inv_std, norm_gain):
    scaled = upstream * norm_gain
    grad_hidden = inv_std * (
        scaled
        - jnp.mean(scaled, -1, keepdims=True)
        - normed * jnp.mean(scaled * normed, -1, keepdims=True)
    )
    return (grad_hidden, jnp.sum(upstream * normed, 0), jnp.sum(upstream, 0))


def feature_map(projected, features):
    head_dim = projected.shape[-1]
    feat_count = features.shape[-1]
    inner_u = jnp.einsum("rthe,hem->rthm", projected, features, preferred_element_type=jnp.float32)
    widened = projected.astype(jnp.float32)
    square = jnp.sum(widened * widened, -1, keepdims=True)
    return jnp.exp(
        inner_u * head_dim ** (-0.25) - 0.5 * head_dim ** (-0.5) * square
    ) * feat_count ** (-0.5)


def feature_back(grad_feat, feat_vals, projected, features):
    head_dim = projected.shape[-1]
    weighted = grad_feat * feat_vals
    grad_inner = (weighted * head_dim ** (-0.25)).astype(jnp.bfloat16)
    grad_proj = jnp.einsum(
        "rthm,hem->rthe", grad_inner, features, preferred_element_type=jnp.float32
    )
    grad_proj = grad_proj - head_dim ** (-0.5) * projected.astype(jnp.float32) * jnp.sum(
        weighted, -1, keepdims=True
    )
    return grad_proj.astype(jnp.bfloat16)


def join_forward(earlier, later):
    earlier_kv, earlier_z, earlier_first, earlier_last, earlier_whole = earlier
    later_kv, later_z, later_first, later_last, later_whole = later
    matched = (earlier_last == later_first) | (earlier_last < 0) | (later_first < 0)
    joined = (later_whole == 1) & matched
    kv_part = jnp.where(joined[:, None, None, None], earlier_kv + later_kv, later_kv)
    z_part = jnp.where(joined[:, None, None], earlier_z + later_z, later_z)
    first_id = jnp.where(earlier_first < 0, later_first, earlier_first)
    last_id = jnp.where(later_last < 0, earlier_last, later_last)
    whole_run = earlier_whole * later_whole * matched.astype(jnp.int32)
    return (kv_part, z_part, first_id, last_id, whole_run)


def join_backward(earlier, later):
    earlier_kv, earlier_z, earlier_first, earlier_last, earlier_whole = earlier
    later_kv, later_z, later_first, later_last, later_whole = later
    matched = (later_last == earlier_first) | (later_last < 0) | (earlier_first < 0)
    joined = (later_whole == 1) & matched
    kv_part = jnp.where(joined[:, None, None, None], earlier_kv + later_kv, later_kv)
    z_part = jnp.where(joined[:, None, None], earlier_z + later_z, later_z)
    first_id = jnp.where(later_first < 0, earlier_first, later_first)
    last_id = jnp.where(earlier_last < 0, later_last, earlier_last)
    whole_run = earlier_whole * later_whole * matched.astype(jnp.int32)
    return (kv_part, z_part, first_id, last_id, whole_run)


def segment_totals(local_kv, local_z, segment_ids):
    row_count = local_kv.shape[0]
    labels = jnp.arange(local_kv.shape[1], dtype=jnp.int32)
    first_id = segment_ids[:, 0]
    last_id = segment_ids[:, -1]
    whole_run = (first_id == last_id).astype(jnp.int32)
    is_last = last_id[:, None] == labels[None, :]
    is_first = first_id[:, None] == labels[None, :]
    tail_kv = jnp.sum(jnp.where(is_last[:, :, None, None, None], local_kv, 0.0), 1)
    tail_z = jnp.sum(jnp.where(is_last[:, :, None, None], local_z, 0.0), 1)
    lead_kv = jnp.sum(jnp.where(is_first[:, :, None, None, None], local_kv, 0.0), 1)
    lead_z = jnp.sum(jnp.where(is_first[:, :, None, None], local_z, 0.0), 1)
    identity = (
        jnp.zeros_like(tail_kv),
        jnp.zeros_like(tail_z),
        -jnp.ones((row_count,), jnp.int32),
        -jnp.ones((row_count,), jnp.int32),
        jnp.ones((row_count,), jnp.int32),
    )
    before = carried_in(
        (tail_kv, tail_z, first_id, last_id, whole_run), "seq", join_forward, identity, False
    )
    behind = carried_in(
        (lead_kv, lead_z, first_id, last_id, whole_run), "seq", join_backward, identity, True
    )
    from_before = before[3][:, None] == labels[None, :]
    from_behind = behind[2][:, None] == labels[None, :]
    total_kv = (
        local_kv
        + jnp.where(from_before[:, :, None, None, None], before[0][:, None], 0.0)
        + jnp.where(from_behind[:, :, None, None, None], behind[0][:, None], 0.0)
    )
    total_z = (
        local_z
        + jnp.where(from_before[:, :, None, None], before[1][:, None], 0.0)
        + jnp.where(from_behind[:, :, None, None], behind[1][:, None], 0.0)
    )
    return (total_kv, total_z)


def body(
    tokens,
    segment_ids,
    features,
    query_weight,
    key_weight,
    value_weight,
    out_weight,
    up_weight,
    down_weight,
    first_gain,
    first_bias,
    second_gain,
    second_bias,
    cotangent,
):
    row_count, row_len, width_d = tokens.shape
    head_count, head_dim = (features.shape[0], features.shape[1])
    token_count = row_count * row_len
    tokens_flat = tokens.reshape(token_count, width_d)

    def project(weight):
        product = jnp.dot(tokens_flat, weight, preferred_element_type=jnp.float32)
        return product.astype(jnp.bfloat16).reshape(row_count, row_len, head_count, head_dim)

    queries = project(query_weight)
    keys_b = project(key_weight)
    values_b = project(value_weight)
    feat_q = feature_map(queries, features)
    feat_k = feature_map(keys_b, features)
    feat_q_b = feat_q.astype(jnp.bfloat16)
    feat_k_b = feat_k.astype(jnp.bfloat16)
    labels = jnp.arange(SEGS, dtype=jnp.int32)
    onehot = segment_ids[:, :, None] == labels[None, None, :]
    mask_b = onehot.astype(jnp.bfloat16)
    mask_f = onehot.astype(jnp.float32)
    masked_values = mask_b[:, :, :, None, None] * values_b[:, :, None]
    local_kv = jnp.einsum(
        "rthm,rtshe->rshme", feat_k_b, masked_values, preferred_element_type=jnp.float32
    )
    local_z = jnp.einsum("rts,rthm->rshm", mask_b, feat_k_b, preferred_element_type=jnp.float32)
    kv_total, z_total = segment_totals(local_kv, local_z, segment_ids)
    kv_b = kv_total.astype(jnp.bfloat16)
    per_segment = jnp.einsum(
        "rthm,rshme->rtshe", feat_q_b, kv_b, preferred_element_type=jnp.float32
    )
    numer = jnp.sum(jnp.where(onehot[:, :, :, None, None], per_segment, 0.0), 2)
    z_picked = jnp.einsum("rts,rshm->rthm", mask_f, z_total, precision=HIGHEST)
    denom = jnp.sum(feat_q_b.astype(jnp.float32) * z_picked, -1)
    attention = numer / denom[..., None]
    attention_b = attention.astype(jnp.bfloat16).reshape(token_count, width_d)
    hidden_one = tokens_flat.astype(jnp.float32) + jnp.dot(
        attention_b, out_weight, preferred_element_type=jnp.float32
    )
    normed_one, unit_one, inv_one = norm_forward(hidden_one, first_gain, first_bias)
    normed_one_b = normed_one.astype(jnp.bfloat16)
    inner_f = jnp.dot(normed_one_b, up_weight, preferred_element_type=jnp.float32)
    activated, gelu_pull = jax.vjp(partial(jax.nn.gelu, approximate=False), inner_f)
    activated_b = activated.astype(jnp.bfloat16)
    hidden_two = normed_one + jnp.dot(activated_b, down_weight, preferred_element_type=jnp.float32)
    result, unit_two, inv_two = norm_forward(hidden_two, second_gain, second_bias)
    upstream = cotangent.reshape(token_count, width_d).astype(jnp.float32)
    grad_two, grad_gain_two, grad_bias_two = norm_backward(upstream, unit_two, inv_two, second_gain)
    grad_branch = grad_two.astype(jnp.bfloat16)
    grad_down_w = jnp.einsum(
        "nf,nd->fd", activated_b, grad_branch, preferred_element_type=jnp.float32
    )
    grad_act = jnp.einsum("nd,fd->nf", grad_branch, down_weight, preferred_element_type=jnp.float32)
    (grad_inner,) = gelu_pull(grad_act)
    grad_inner_b = grad_inner.astype(jnp.bfloat16)
    grad_up_w = jnp.einsum(
        "nd,nf->df", normed_one_b, grad_inner_b, preferred_element_type=jnp.float32
    )
    grad_normed = grad_two + jnp.einsum(
        "nf,df->nd", grad_inner_b, up_weight, preferred_element_type=jnp.float32
    )
    grad_one, grad_gain_one, grad_bias_one = norm_backward(
        grad_normed, unit_one, inv_one, first_gain
    )
    grad_attn_out = grad_one.astype(jnp.bfloat16)
    grad_out_w = jnp.einsum(
        "nd,ne->de", attention_b, grad_attn_out, preferred_element_type=jnp.float32
    )
    grad_attention = jnp.einsum(
        "ne,de->nd", grad_attn_out, out_weight, preferred_element_type=jnp.float32
    )
    grad_attention = grad_attention.reshape(row_count, row_len, head_count, head_dim)
    grad_numer_b = (grad_attention / denom[..., None]).astype(jnp.bfloat16)
    grad_denom = -jnp.sum(grad_attention * attention, -1) / denom
    masked_grad = mask_b[:, :, :, None, None] * grad_numer_b[:, :, None]
    grad_feat_q = jnp.einsum(
        "rtshe,rshme->rthm", masked_grad, kv_b, preferred_element_type=jnp.float32
    )
    grad_feat_q = grad_feat_q + z_picked * grad_denom[..., None]
    local_grad_kv = jnp.einsum(
        "rthm,rtshe->rshme", feat_q_b, masked_grad, preferred_element_type=jnp.float32
    )
    local_grad_z = jnp.einsum(
        "rts,rthm->rshm",
        mask_f,
        feat_q_b.astype(jnp.float32) * grad_denom[..., None],
        precision=HIGHEST,
    )
    grad_kv_total, grad_z_total = segment_totals(local_grad_kv, local_grad_z, segment_ids)
    grad_kv_b = grad_kv_total.astype(jnp.bfloat16)
    grad_feat_k = jnp.einsum(
        "rtshe,rshme->rthm", masked_values, grad_kv_b, preferred_element_type=jnp.float32
    )
    grad_feat_k = grad_feat_k + jnp.einsum(
        "rts,rshm->rthm", mask_f, grad_z_total, precision=HIGHEST
    )
    value_terms = jnp.einsum(
        "rthm,rshme->rtshe", feat_k_b, grad_kv_b, preferred_element_type=jnp.float32
    )
    grad_values = jnp.sum(jnp.where(onehot[:, :, :, None, None], value_terms, 0.0), 2).astype(
        jnp.bfloat16
    )
    grad_queries = feature_back(grad_feat_q, feat_q, queries, features)
    grad_keys = feature_back(grad_feat_k, feat_k, keys_b, features)
    grad_q_flat = grad_queries.reshape(token_count, width_d)
    grad_k_flat = grad_keys.reshape(token_count, width_d)
    grad_v_flat = grad_values.reshape(token_count, width_d)
    grad_query_w = jnp.einsum(
        "nd,ne->de", tokens_flat, grad_q_flat, preferred_element_type=jnp.float32
    )
    grad_key_w = jnp.einsum(
        "nd,ne->de", tokens_flat, grad_k_flat, preferred_element_type=jnp.float32
    )
    grad_value_w = jnp.einsum(
        "nd,ne->de", tokens_flat, grad_v_flat, preferred_element_type=jnp.float32
    )
    grad_input = (
        grad_one
        + jnp.einsum("ne,de->nd", grad_q_flat, query_weight, preferred_element_type=jnp.float32)
        + jnp.einsum("ne,de->nd", grad_k_flat, key_weight, preferred_element_type=jnp.float32)
        + jnp.einsum("ne,de->nd", grad_v_flat, value_weight, preferred_element_type=jnp.float32)
    )
    local_grads = (
        grad_query_w,
        grad_key_w,
        grad_value_w,
        grad_out_w,
        grad_up_w,
        grad_down_w,
        grad_gain_one,
        grad_bias_one,
        grad_gain_two,
        grad_bias_two,
    )
    shares = (
        lax.psum_scatter(local_grads[0], "seq", scatter_dimension=0, tiled=True),
        lax.psum_scatter(local_grads[1], "seq", scatter_dimension=0, tiled=True),
        lax.psum_scatter(local_grads[2], "seq", scatter_dimension=0, tiled=True),
        lax.psum_scatter(local_grads[3], "seq", scatter_dimension=0, tiled=True),
        lax.psum_scatter(local_grads[4], "seq", scatter_dimension=0, tiled=True),
        lax.psum_scatter(local_grads[5], "seq", scatter_dimension=0, tiled=True),
        lax.psum_scatter(local_grads[6], "seq", scatter_dimension=0, tiled=True),
        lax.psum_scatter(local_grads[7], "seq", scatter_dimension=0, tiled=True),
        lax.psum_scatter(local_grads[8], "seq", scatter_dimension=0, tiled=True),
        lax.psum_scatter(local_grads[9], "seq", scatter_dimension=0, tiled=True),
    )
    shares = lax.psum(
        (
            shares[0],
            shares[1],
            shares[2],
            shares[3],
            shares[4],
            shares[5],
            shares[6],
            shares[7],
            shares[8],
            shares[9],
        ),
        "dp",
    )
    summed = (
        lax.all_gather(shares[0], "seq", axis=0, tiled=True),
        lax.all_gather(shares[1], "seq", axis=0, tiled=True),
        lax.all_gather(shares[2], "seq", axis=0, tiled=True),
        lax.all_gather(shares[3], "seq", axis=0, tiled=True),
        lax.all_gather(shares[4], "seq", axis=0, tiled=True),
        lax.all_gather(shares[5], "seq", axis=0, tiled=True),
        lax.all_gather(shares[6], "seq", axis=0, tiled=True),
        lax.all_gather(shares[7], "seq", axis=0, tiled=True),
        lax.all_gather(shares[8], "seq", axis=0, tiled=True),
        lax.all_gather(shares[9], "seq", axis=0, tiled=True),
    )
    return (
        result.astype(jnp.bfloat16).reshape(row_count, row_len, width_d),
        grad_input.astype(jnp.bfloat16).reshape(row_count, row_len, width_d),
        summed[0],
        summed[1],
        summed[2],
        summed[3],
        summed[4],
        summed[5],
        summed[6],
        summed[7],
        summed[8],
        summed[9],
    )


def solution(mesh):
    placed = (
        P("dp", "seq", None),
        P("dp", "seq"),
        P(),
        P(),
        P(),
        P(),
        P(),
        P(),
        P(),
        P(),
        P(),
        P(),
        P(),
        P("dp", "seq", None),
    )
    return jax.shard_map(
        body,
        mesh=mesh,
        in_specs=placed,
        out_specs=(
            P("dp", "seq", None),
            P("dp", "seq", None),
            P(),
            P(),
            P(),
            P(),
            P(),
            P(),
            P(),
            P(),
            P(),
            P(),
        ),
        check_vma=False,
    )
```

profile of v0, /device:TPU:0, one launch (start us, length us, event | category | flops | bytes accessed | tf_op | source)
XLA Modules:
  0.0 1851.2 jit_solution(2164421294902823707)
XLA Ops:
  17.5 5.5 fusion.14
  29.0 14.8 all-reduce.11
  51.6 21.3 %all-gather.9 = f32[16,12,256]{2,1,0:T(8,128)} all-gather(f32[1,12,256]{2,1,0:T(8,128)S(1)} %bitcast.471), channel_id=5, replica_groups=mesh['dp'=2,'seq'=16] {'seq'}, dimensions={0}, use_global_device_ids=true | all-gather | bytes 208896 | tf_op jit(solution)/shard_map/all_gather | solution.py:14
  72.9 22.4 %all-gather.8 = f32[16,12,256]{2,1,0:T(8,128)} all-gather(f32[1,12,256]{2,1,0:T(8,128)S(1)} %bitcast.470), channel_id=3, replica_groups=mesh['dp'=2,'seq'=16] {'seq'}, dimensions={0}, use_global_device_ids=true | all-gather | bytes 208896 | tf_op jit(solution)/shard_map/all_gather | solution.py:14
  98.3 31.5 %all-gather.37.cloned.1.call-done = f32[192,256,64]{1,2,0:T(8,128)} async-done(((f32[12,256,64]{1,2,0:T(8,128)}), f32[192,256,64]{1,2,0:T(8,128)}) %all-gather.37.cloned.1.call-update) | async-done | bytes 12582928 | tf_op jit(solution)/shard_map/all_gather | solution.py:14
  129.8 174.6 %while.77 = (s32[]{:T(128)}, f32[1,12,256,64]{3,2,1,0:T(8,128)}, f32[1,12,256]{2,1,0:T(8,128)}, s32[1]{0:T(128)}, s32[]{:T(128)}, /*index=5*/s32[16,1]{0,1:T(1,1...) while((s32[]{:T(128)}, f32[1,12,256,64]{3,2,1,0:T(8,128)}, ...), condition=%wide.region_8.9_spmd.clone, body=%wide.region_7.8_spmd.clone.sunk | while | flops 798738 | bytes 5640575 | solution.py:27
  156.5 2.8 fusion.225
  167.5 2.8 fusion.225
  178.7 2.8 fusion.225
  222.6 2.9 fusion.225
  233.8 2.8 fusion.225
  277.6 2.8 fusion.225
  288.6 2.8 fusion.225
  307.1 173.8 %while.76 = (s32[]{:T(128)}, f32[1,12,256,64]{3,2,1,0:T(8,128)}, f32[1,12,256]{2,1,0:T(8,128)S(1)}, s32[1]{0:T(128)}, s32[]{:T(128)}, /*index=5*/s32[16,1]{0,1:T...) while((s32[]{:T(128)}, f32[1,12,256,64]{3,2,1,0:T(8,128)}, ...), condition=%wide.region_4.5_spmd.clone, body=%wide.region_3.4_spmd.clone.sunk | while | flops 798734 | bytes 5542153 | solution.py:27
  322.8 2.8 fusion.222
  333.7 2.8 fusion.222
  482.9 4.4 fusion.31
  487.4 3.7 fusion.26
  494.2 8.1 multiply_convert_fusion.2
  506.0 3.6 add_convert_fusion
  514.0 5.5 fusion.10
  520.4 5.8 fusion.172
  529.3 3.5 copy.120
  535.2 22.8 %all-gather.11 = f32[16,12,256]{2,1,0:T(8,128)} all-gather(f32[1,12,256]{2,1,0:T(8,128)S(1)} %bitcast.469), channel_id=9, replica_groups=mesh['dp'=2,'seq'=16] {'seq'}, dimensions={0}, use_global_device_ids=true | all-gather | bytes 208896 | tf_op jit(solution)/shard_map/all_gather | solution.py:14
  558.1 20.8 %all-gather.10 = f32[16,12,256]{2,1,0:T(8,128)} all-gather(f32[1,12,256]{2,1,0:T(8,128)S(1)} %bitcast.468), channel_id=7, replica_groups=mesh['dp'=2,'seq'=16] {'seq'}, dimensions={0}, use_global_device_ids=true | all-gather | bytes 208896 | tf_op jit(solution)/shard_map/all_gather | solution.py:14
  578.9 41.9 %all-gather.41.cloned.1.call-done = f32[192,256,64]{1,2,0:T(8,128)} async-done(((f32[12,256,64]{1,2,0:T(8,128)}), f32[192,256,64]{1,2,0:T(8,128)}) %all-gather.41.cloned.1.call-update) | async-done | bytes 12582928 | tf_op jit(solution)/shard_map/all_gather | solution.py:14
  620.8 172.1 %while.79 = (s32[]{:T(128)}, f32[1,12,256,64]{3,2,1,0:T(8,128)}, f32[1,12,256]{2,1,0:T(8,128)}, s32[1]{0:T(128)}, s32[]{:T(128)}, /*index=5*/s32[16,1]{0,1:T(1,1...) while((s32[]{:T(128)}, f32[1,12,256,64]{3,2,1,0:T(8,128)}, ...), condition=%wide.region_29.30_spmd.clone, body=%wide.region_28.29_spmd.clone.sunk | while | flops 798738 | bytes 5640575 | solution.py:27
  636.3 2.8 fusion.231
  647.1 2.8 fusion.231
  658.0 2.8 fusion.231
  668.8 2.8 fusion.231
  679.6 2.8 fusion.231
  690.5 2.8 fusion.231
  701.3 2.9 fusion.231
  712.2 2.8 fusion.231
  723.0 2.8 fusion.231
  733.9 2.8 fusion.231
  744.8 2.8 fusion.231
  755.6 2.8 fusion.231
  766.5 2.8 fusion.231
  777.3 2.8 fusion.231
  788.1 2.8 fusion.231
  793.0 171.2 %while.78 = (s32[]{:T(128)}, f32[1,12,256,64]{3,2,1,0:T(8,128)}, f32[1,12,256]{2,1,0:T(8,128)S(1)}, s32[1]{0:T(128)}, s32[]{:T(128)}, /*index=5*/s32[16,1]{0,1:T...) while((s32[]{:T(128)}, f32[1,12,256,64]{3,2,1,0:T(8,128)}, ...), condition=%wide.region_25.26_spmd.clone, body=%wide.region_24.25_spmd.clone.sunk | while | flops 798734 | bytes 5542153 | solution.py:27
  970.1 4.2 fusion.32
  979.2 3.2 copy.122
  982.4 2.9 fusion.8
  987.9 3.2 copy.124
  993.4 6.8 fusion.156
  1002.0 6.0 fusion.116
  1010.0 34.8 %reduce-scatter.21.cloned.1.call-done = f32[48,768]{1,0:T(8,128)} async-done(((f32[768,768]{1,0:T(8,128)}), f32[48,768]{1,0:T(8,128)}) %reduce-scatter.21.cloned.1.call-update) | async-done | bytes 147472
  1046.7 64.7 %reduce-scatter.23.cloned.1.call-done = f32[48,768]{1,0:T(8,128)} async-done(((f32[768,768]{1,0:T(8,128)}), f32[48,768]{1,0:T(8,128)}) %reduce-scatter.23.cloned.1.call-update) | async-done | bytes 147472
  1113.2 64.7 %reduce-scatter.13.cloned.1.call-done = f32[48,768]{1,0:T(8,128)} async-done(((f32[768,768]{1,0:T(8,128)}), f32[48,768]{1,0:T(8,128)}) %reduce-scatter.13.cloned.1.call-update) | async-done | bytes 147472 | tf_op jit(solution)/shard_map/reduce_scatter | solution.py:292
  1177.9 115.0 %reduce-scatter.15.cloned.1.call-done = f32[48,3072]{1,0:T(8,128)} async-done(((f32[768,3072]{1,0:T(8,128)}), f32[48,3072]{1,0:T(8,128)}) %reduce-scatter.15.cloned.1.call-update) | async-done | bytes 589840 | tf_op jit(solution)/shard_map/reduce_scatter | solution.py:293
  1292.8 115.4 %reduce-scatter.17.cloned.1.call-done = f32[192,768]{1,0:T(8,128)} async-done(((f32[3072,768]{1,0:T(8,128)}), f32[192,768]{1,0:T(8,128)}) %reduce-scatter.17.cloned.1.call-update) | async-done | bytes 589840 | tf_op jit(solution)/shard_map/reduce_scatter | solution.py:294
  1408.3 74.8 %all-reduce.18.cloned.1.call-done = (f32[48,768]{0,1:T(8,128)}, f32[48,768]{0,1:T(8,128)}, f32[48,768]{0,1:T(8,128)}, f32[48,768]{1,0:T(8,128)}, f32[48,3072]{1,0:T(8,128)}, /*index=5*/f32[192,768]{1,0:T(8,128)}) async-done(((f32[48,768]{0,1:T(8,128)}, f32[48,768]{0,1:T(8,128)}, f32[48,768]{0,1:T(8,128)}, f32[48,768]{1,0:T(8,128)}, f32[48,3072]{1,0:T(8,128)}, /*index=5*/f32[192,768]{1,0:T(8,128)}), ...) | async-done | bytes 1769488 | tf_op jit(solution)/shard_map/psum | solution.py:300
  1492.9 61.7 %all-reduce.13 = (f32[768]{0:T(1024)}, f32[768]{0:T(1024)}, f32[768]{0:T(1024)}, f32[768]{0:T(1024)}) all-reduce(f32[768]{0:T(1024)S(1)} %copy-done.94, f32[768]{0:T(1024)S(1)} %copy-done.95, f32[768]{0:T(1024)S(1)} %copy-done.76, f32[768]{0:T(1024)S(1)} %convert_reduce_fusion), channel_id=16, replica_groups=mesh['dp'=2,'seq'=16] {'seq'}, use_global_device_ids=true, to_apply=%region_45.46.clone | all-reduce | flops 3072 | bytes 24576
  1557.6 5.4 all-reduce.14
  1566.4 58.2 %all-reduce.12 = (f32[768]{0:T(1024)}, f32[768]{0:T(1024)}, f32[768]{0:T(1024)}, f32[768]{0:T(1024)}) all-reduce(f32[768]{0:T(1024)S(1)} %dynamic-update-slice.3, f32[768]{0:T(1024)S(1)} %dynamic-update-slice.4, f32[768]{0:T(1024)S(1)} %dynamic-update-slice.5, f32[768]{0:T(1024)S(1)} %dynamic-update-slice.6), channel_id=1, replica_groups=mesh['dp'=2,'seq'=16] {'seq'}, use_global_device_ids=true, to_apply=%add.3 | all-reduce | flops 3072 | bytes 24576
  1627.4 32.4 %all-gather.29.cloned.1.call-done = f32[768,768]{1,0:T(8,128)} async-done(((f32[48,768]{1,0:T(8,128)}), f32[768,768]{1,0:T(8,128)}) %all-gather.29.cloned.1.call-update) | async-done | bytes 2359312 | tf_op jit(solution)/shard_map/all_gather | solution.py:319
  1659.7 81.8 %all-gather.31.cloned.1.call-done = f32[768,3072]{1,0:T(8,128)} async-done(((f32[48,3072]{1,0:T(8,128)}), f32[768,3072]{1,0:T(8,128)}) %all-gather.31.cloned.1.call-update) | async-done | bytes 9437200 | tf_op jit(solution)/shard_map/all_gather | solution.py:320
  1741.5 81.5 %all-gather.33.cloned.1.call-done = f32[3072,768]{1,0:T(8,128)} async-done(((f32[192,768]{1,0:T(8,128)}), f32[3072,768]{1,0:T(8,128)}) %all-gather.33.cloned.1.call-update) | async-done | bytes 9437200 | tf_op jit(solution)/shard_map/all_gather | solution.py:321
  1823.0 3.4 copy.211
  1832.6 3.7 copy.215
  1836.4 8.1 copy.216
  (826 shorter events, 513.9 us)
Async XLA Ops:
  7.2 485.1 %copy-start = (bf16[768,768]{1,0:T(8,128)(2,1)S(1)}, bf16[768,768]{1,0:T(8,128)(2,1)}, u32[]{:S(2)}) copy-start(bf16[768,768]{1,0:T(8,128)(2,1)} %param.28) | copy-start | bytes 3538948
  7.2 122.6 %all-gather.37.cloned.1.call-start = ((), (), s32[]{:S(2)}) async-start(), calls=%async_computation.16 | async-start | bytes 13369344 | tf_op jit(solution)/shard_map/all_gather | solution.py:14
  9.4 8.0 copy-start.13
  15.0 8.0 copy-start.81
  15.0 8.0 copy-start.84
  17.5 7.7 copy-start.98
  23.0 26.7 %copy-start.18 = (bf16[1,256,12,256]{1,3,2,0:T(8,128)(2,1)S(1)}, bf16[1,256,12,256]{1,3,2,0:T(8,128)(2,1)}, u32[]{:S(2)}) copy-start(bf16[1,256,12,256]{1,3,2,0:T(8,128)(2,1)} %copy-done.17) | copy-start | bytes 4718596
  23.0 284.1 %all-gather.35.cloned.1.call-start = ((), (), s32[]{:S(2)}) async-start(), calls=%async_computation.15 | async-start | bytes 13369344 | tf_op jit(solution)/shard_map/all_gather | solution.py:14
  23.8 597.0 %all-gather.41.cloned.1.call-start = ((), (), s32[]{:S(2)}) async-start(), calls=%async_computation.18 | async-start | bytes 13369344 | tf_op jit(solution)/shard_map/all_gather | solution.py:14
  47.5 50.8 %copy-start.15 = (f32[256,768]{0,1:T(8,128)}, f32[256,768]{0,1:T(8,128)S(1)}, u32[]{:S(2)}) copy-start(f32[256,768]{0,1:T(8,128)S(1)} %copy.83) | copy-start | bytes 2359300
  49.7 46.3 %copy-start.23 = (bf16[12,64,256]{2,1,0:T(8,128)(2,1)S(1)}, bf16[12,64,256]{2,1,0:T(8,128)(2,1)}, u32[]{:S(2)}) copy-start(bf16[12,64,256]{2,1,0:T(8,128)(2,1)} %param.24) | copy-start | bytes 1179652
  49.7 46.3 %copy-start.46 = (bf16[256,768]{0,1:T(8,128)(2,1)S(1)}, bf16[256,768]{0,1:T(8,128)(2,1)}, u32[]{:S(2)}) copy-start(bf16[256,768]{0,1:T(8,128)(2,1)} %copy.82) | copy-start | bytes 1179652
  141.1 7.2 copy-start.49
  152.1 7.3 copy-start.49
  163.0 7.2 copy-start.49
  174.2 7.3 copy-start.49
  185.2 7.2 copy-start.49
  196.2 7.2 copy-start.49
  207.2 7.2 copy-start.49
  218.2 7.4 copy-start.49
  229.3 7.2 copy-start.49
  240.3 7.2 copy-start.49
  251.2 7.2 copy-start.49
  262.2 7.2 copy-start.49
  273.2 7.2 copy-start.49
  284.1 7.2 copy-start.49
  295.1 7.2 copy-start.49
  491.1 22.8 %copy-start.52 = (f32[256,12]{0,1:T(8,128)}, f32[256,12]{0,1:T(8,128)S(1)}, u32[]{:S(2)}) copy-start(f32[256,12]{0,1:T(8,128)S(1)} %get-tuple-element.1168) | copy-start | bytes 36868
  491.1 22.9 %copy-start.20 = (bf16[1,256,12,256]{1,3,2,0:T(8,128)(2,1)}, bf16[1,256,12,256]{1,3,2,0:T(8,128)(2,1)S(1)}, u32[]{:S(2)}) copy-start(bf16[1,256,12,256]{1,3,2,0:T(8,128)(2,1)S(1)} %get-tuple-element.1169) | copy-start | bytes 4718596
  492.5 9.8 slice-start
  493.1 19.0 %copy-start.8 = (f32[256,768]{1,0:T(8,128)}, f32[256,768]{1,0:T(8,128)S(1)}, u32[]{:S(2)}) copy-start(f32[256,768]{1,0:T(8,128)S(1)} %get-tuple-element.1191) | copy-start | bytes 2359300
  493.1 19.0 %copy-start.70 = (f32[256]{0:T(256)}, f32[256]{0:T(256)S(1)}, u32[]{:S(2)}) copy-start(f32[256]{0:T(256)S(1)} %broadcast_multiply_fusion.9) | copy-start | bytes 3076
  494.2 17.9 copy-start.77
  494.2 8.2 slice-start.1
  519.5 273.4 %all-gather.39.cloned.1.call-start = ((), (), s32[]{:S(2)}) async-start(), calls=%async_computation.17 | async-start | bytes 13369344 | tf_op jit(solution)/shard_map/all_gather | solution.py:14
  520.1 488.1 %reduce-scatter.19.cloned.1.call-start = ((), (), s32[]{:S(2)}) async-start(), calls=%async_computation.19 | async-start | bytes 2506752
  578.9 466.0 %reduce-scatter.21.cloned.1.call-start = ((), (), s32[]{:S(2)}) async-start(), calls=%async_computation.20 | async-start | bytes 2506752
  642.8 7.1 copy-start.47
  664.5 7.1 copy-start.47
  675.3 7.1 copy-start.47
  697.0 7.2 copy-start.47
  707.9 7.1 copy-start.47
  729.5 7.2 copy-start.47
  762.1 7.1 copy-start.47
  783.8 7.1 copy-start.47
  982.3 129.0 %reduce-scatter.23.cloned.1.call-start = ((), (), s32[]{:S(2)}) async-start(), calls=%async_computation.21 | async-start | bytes 2506752
  991.2 186.7 %reduce-scatter.13.cloned.1.call-start = ((), (), s32[]{:S(2)}) async-start(), calls=%async_computation.9 | async-start | bytes 2506752 | tf_op jit(solution)/shard_map/reduce_scatter | solution.py:292
  993.3 299.5 %reduce-scatter.15.cloned.1.call-start = ((), (), s32[]{:S(2)}) async-start(), calls=%async_computation.11 | async-start | bytes 10027008 | tf_op jit(solution)/shard_map/reduce_scatter | solution.py:293
  1000.3 407.9 %reduce-scatter.17.cloned.1.call-start = ((), (), s32[]{:S(2)}) async-start(), calls=%async_computation.13 | async-start | bytes 10027008 | tf_op jit(solution)/shard_map/reduce_scatter | solution.py:294
  1008.1 475.0 %all-reduce.18.cloned.1.call-start = ((), (), s32[]{:S(2)}) async-start(), calls=%async_computation.22 | async-start | bytes 5013504 | tf_op jit(solution)/shard_map/psum | solution.py:300
  1408.2 84.6 %copy-start.76 = (f32[768]{0:T(1024)S(1)}, f32[768]{0:T(1024)}, u32[]{:S(2)}) copy-start(f32[768]{0:T(1024)} %get-tuple-element.1056) | copy-start | bytes 9220
  1408.2 84.6 %copy-start.94 = (f32[768]{0:T(1024)S(1)}, f32[768]{0:T(1024)}, u32[]{:S(2)}) copy-start(f32[768]{0:T(1024)} %get-tuple-element.1054) | copy-start | bytes 9220
  1408.2 84.7 %copy-start.95 = (f32[768]{0:T(1024)S(1)}, f32[768]{0:T(1024)}, u32[]{:S(2)}) copy-start(f32[768]{0:T(1024)} %get-tuple-element.1059) | copy-start | bytes 9220
  1408.2 216.3 %copy-start.25 = (bf16[768,768]{1,0:T(8,128)(2,1)S(1)}, bf16[768,768]{1,0:T(8,128)(2,1)}, u32[]{:S(2)}) copy-start(bf16[768,768]{1,0:T(8,128)(2,1)} %param.25) | copy-start | bytes 3538948
  1408.2 216.3 %copy-start.29 = (bf16[1,256,12,64]{1,3,2,0:T(8,128)(2,1)S(1)}, bf16[1,256,12,64]{1,3,2,0:T(8,128)(2,1)}, u32[]{:S(2)}) copy-start(bf16[1,256,12,64]{1,3,2,0:T(8,128)(2,1)} %copy-done.28) | copy-start | bytes 1179652
  1408.3 219.1 %all-gather.23.cloned.1.call-start = ((), (), s32[]{:S(2)}) async-start(), calls=%async_computation.6 | async-start | bytes 2506752 | tf_op jit(solution)/shard_map/all_gather | solution.py:316
  1484.9 142.4 %all-gather.25.cloned.1.call-start = ((), (), s32[]{:S(2)}) async-start(), calls=%async_computation.7 | async-start | bytes 2506752 | tf_op jit(solution)/shard_map/all_gather | solution.py:317
  1485.0 140.1 %copy-start.26 = (bf16[768,768]{1,0:T(8,128)(2,1)S(1)}, bf16[768,768]{1,0:T(8,128)(2,1)}, u32[]{:S(2)}) copy-start(bf16[768,768]{1,0:T(8,128)(2,1)} %param.26) | copy-start | bytes 3538948
  1486.9 140.5 %all-gather.27.cloned.1.call-start = ((), (), s32[]{:S(2)}) async-start(), calls=%async_computation.8 | async-start | bytes 2506752 | tf_op jit(solution)/shard_map/all_gather | solution.py:318
  1488.8 170.9 %all-gather.29.cloned.1.call-start = ((), (), s32[]{:S(2)}) async-start(), calls=%async_computation.10 | async-start | bytes 2506752 | tf_op jit(solution)/shard_map/all_gather | solution.py:319
  1489.4 252.1 %all-gather.31.cloned.1.call-start = ((), (), s32[]{:S(2)}) async-start(), calls=%async_computation.12 | async-start | bytes 10027008 | tf_op jit(solution)/shard_map/all_gather | solution.py:320
  1490.0 333.0 %all-gather.33.cloned.1.call-start = ((), (), s32[]{:S(2)}) async-start(), calls=%async_computation.14 | async-start | bytes 10027008 | tf_op jit(solution)/shard_map/all_gather | solution.py:321
  1627.4 199.0 %copy-start.40 = (f32[768,768]{1,0:T(8,128)S(1)}, f32[768,768]{1,0:T(8,128)}, u32[]{:S(2)}) copy-start(f32[768,768]{1,0:T(8,128)} %all-gather.25.cloned.1.call-done) | copy-start | bytes 7077892
  1836.4 8.1 copy-start.1
  (116 other events, 343.6 us)
Sparse Core Ops, SparseCore 0:
  23.1 106.5 all-gather.36
  132.6 98.5 all-gather.34
  519.7 101.1 all-gather.40
  622.9 99.1 all-gather.38
  726.3 61.6 reduce-scatter.18
  982.5 62.3 reduce-scatter.20
  1049.2 62.1 reduce-scatter.22
  1115.7 62.1 reduce-scatter.12
  1182.6 110.2 reduce-scatter.14
  1297.4 110.8 reduce-scatter.16
  1411.4 71.6 all-reduce.17
  1485.8 42.5 all-gather.22
  1531.3 41.1 all-gather.24
  1575.2 41.1 all-gather.26
  1618.6 41.1 all-gather.28
  1661.9 79.6 all-gather.30
  1743.6 79.3 all-gather.32
where the time goes:
time: 1870 us; the launch traced here: 1850 us
  waiting for transfers between devices  741 us (40%)
  other arithmetic  311 us (17%)
  local copies, waits for them, and re-layouts  263 us (14%)
  blocking collectives  227 us (12%)
  loops' own time  205 us (11%)
  matrix products  84.1 us (4%)
    select_n x128, other arithmetic, hop(): return jax.tree.map(lambda a, b: jnp.where(reached, a, b), new, before)  219 us
    another operation x4, loops' own time, carried_in(): return lax.fori_loop(0, length, hop, start)  205 us
    dynamic_slice x192, local copies, waits for them, and re-layouts, hop(): new = combine(before, jax.tree.map(lambda part: part[at], everything))  191 us
    unnamed x3, blocking collectives  135 us
    reduce_scatter x1, waiting for transfers between devices, body(): lax.psum_scatter(local_grads[5], 'seq', scatter_dimension=0, tiled=True)  115 us
    reduce_scatter x1, waiting for transfers between devices, body(): lax.psum_scatter(local_grads[4], 'seq', scatter_dimension=0, tiled=True)  115 us
    unnamed x20, waiting for transfers between devices  103 us
    all_gather x4, blocking collectives, carried_in(): everything = jax.tree.map(lambda part: lax.all_gather(part, axis), value)  87.3 us
  transfers between devices with their start and end apart: 17, of which 11 were waited for; matrix products, arithmetic and copies ran while one was open for 25% of the time, Pallas kernels for 0%

commit v1 on v0

--- a/solution.py
+++ b/solution.py
@@ -7,6 +7,22 @@
 SEGS = 8
 EPSILON = 1e-06
 HIGHEST = lax.Precision.HIGHEST
+
+
+def gather_around(x, axis, dim):
+    ways, here, hop = (lax.axis_size(axis), lax.axis_index(axis), x.shape[dim])
+    lengths = [n * ways if d == dim else n for d, n in enumerate(x.shape)]
+    full = lax.dynamic_update_slice_in_dim(jnp.zeros(lengths, x.dtype), x, here * hop, axis=dim)
+    going_up = going_down = x
+    for far in range(1, ways // 2 + 1):
+        going_up = lax.ppermute(going_up, axis, [(d, (d + 1) % ways) for d in range(ways)])
+        full = lax.dynamic_update_slice_in_dim(full, going_up, (here - far) % ways * hop, axis=dim)
+        if 2 * far < ways:
+            going_down = lax.ppermute(going_down, axis, [(d, (d - 1) % ways) for d in range(ways)])
+            full = lax.dynamic_update_slice_in_dim(
+                full, going_down, (here + far) % ways * hop, axis=dim
+            )
+    return full
 
 
 def carried_in(value, axis, combine, identity, reverse):
@@ -318,7 +334,7 @@
         lax.all_gather(shares[2], "seq", axis=0, tiled=True),
         lax.all_gather(shares[3], "seq", axis=0, tiled=True),
         lax.all_gather(shares[4], "seq", axis=0, tiled=True),
-        lax.all_gather(shares[5], "seq", axis=0, tiled=True),
+        gather_around(shares[5], "seq", 0),
         lax.all_gather(shares[6], "seq", axis=0, tiled=True),
         lax.all_gather(shares[7], "seq", axis=0, tiled=True),
         lax.all_gather(shares[8], "seq", axis=0, tiled=True),

time: 1870 us -> 1820 us (0.973)
  waiting for transfers between devices: 741 us -> 635 us
  starting transfers between devices: 0.86 us -> 38 us
    all_gather x1 -> x0, waiting for transfers between devices: 81.5 us -> none  [body(): lax.all_gather(shares[5], 'seq', axis=0, tiled=True)]
    ppermute x0 -> x15, waiting for transfers between devices: none -> 66.4 us  [the longest x8 48.3 us: gather_around(): lax.ppermute(going_up, axis, [(d, (d + 1) % ways) for d in range(ways)])]
    all_gather x1, waiting for transfers between devices: 81.8 us -> 23.5 us  [body(): lax.all_gather(shares[4], 'seq', axis=0, tiled=True)]
    ppermute x0 -> x15, starting transfers between devices: none -> 37.2 us  [the longest x8 21.3 us: gather_around(): lax.ppermute(going_up, axis, [(d, (d + 1) % ways) for d in range(ways)])]
    all_gather x1, waiting for transfers between devices: 32.4 us -> 0.02 us  [body(): lax.all_gather(shares[3], 'seq', axis=0, tiled=True)]
    dynamic_update_slice x0 -> x16, local copies, waits for them, and re-layouts: none -> 21.3 us  [the longest x8 11.3 us: gather_around(): lax.dynamic_update_slice_in_dim(full, going_up, (here - far) % ways * hop...]
    unnamed x229 -> x236, local copies, waits for them, and re-layouts: 53.8 us -> 40.9 us
    unnamed x20 -> x19, waiting for transfers between devices: 103 us -> 101 us
  transfers between devices with their start and end apart: 17 -> 31, of which waited for: 11 -> 17; matrix products, arithmetic and copies ran while one was open for 25% -> 27% of each run, Pallas kernels for 0% -> 0%
where the time goes in v1:
time: 1820 us; the launch traced here: 1800 us
  waiting for transfers between devices  635 us (35%)
  other arithmetic  317 us (17%)
  local copies, waits for them, and re-layouts  276 us (15%)
  blocking collectives  226 us (12%)
  loops' own time  203 us (11%)
  matrix products  87.6 us (5%)
  starting transfers between devices  38 us (2%)
  between operations  18.2 us (1%)
    select_n x128, other arithmetic, hop(): return jax.tree.map(lambda a, b: jnp.where(reached, a, b), new, before)  221 us
    another operation x4, loops' own time, carried_in(): return lax.fori_loop(0, length, hop, start)  203 us
    dynamic_slice x192, local copies, waits for them, and re-layouts, hop(): new = combine(before, jax.tree.map(lambda part: part[at], everything))  190 us
    unnamed x3, blocking collectives  134 us
    reduce_scatter x1, waiting for transfers between devices, body(): lax.psum_scatter(local_grads[5], 'seq', scatter_dimension=0, tiled=True)  115 us
    reduce_scatter x1, waiting for transfers between devices, body(): lax.psum_scatter(local_grads[4], 'seq', scatter_dimension=0, tiled=True)  115 us
    unnamed x19, waiting for transfers between devices  101 us
    all_gather x4, blocking collectives, carried_in(): everything = jax.tree.map(lambda part: lax.all_gather(part, axis), value)  87.7 us
  transfers between devices with their start and end apart: 31, of which 17 were waited for; matrix products, arithmetic and copies ran while one was open for 27% of the time, Pallas kernels for 0%

profile of v1, /device:TPU:0, one launch (start us, length us, event | category | flops | bytes accessed | tf_op | source)
XLA Modules:
  0.0 1800.8 jit_solution(6635582913711101667)
XLA Ops:
  17.5 5.5 fusion.14
  29.0 14.7 all-reduce.11
  51.6 21.3 %all-gather.9 = f32[16,12,256]{2,1,0:T(8,128)} all-gather(f32[1,12,256]{2,1,0:T(8,128)S(1)} %bitcast.471), channel_id=5, replica_groups=mesh['dp'=2,'seq'=16] {'seq'}, dimensions={0}, use_global_device_ids=true | all-gather | bytes 208896 | tf_op jit(solution)/shard_map/all_gather | solution.py:30
  72.9 22.4 %all-gather.8 = f32[16,12,256]{2,1,0:T(8,128)} all-gather(f32[1,12,256]{2,1,0:T(8,128)S(1)} %bitcast.470), channel_id=3, replica_groups=mesh['dp'=2,'seq'=16] {'seq'}, dimensions={0}, use_global_device_ids=true | all-gather | bytes 208896 | tf_op jit(solution)/shard_map/all_gather | solution.py:30
  98.3 31.4 %all-gather.34.cloned.1.call-done = f32[192,256,64]{1,2,0:T(8,128)} async-done(((f32[12,256,64]{1,2,0:T(8,128)}), f32[192,256,64]{1,2,0:T(8,128)}) %all-gather.34.cloned.1.call-update) | async-done | bytes 12582928 | tf_op jit(solution)/shard_map/all_gather | solution.py:30
  129.8 172.8 %while.77 = (s32[]{:T(128)}, f32[1,12,256,64]{3,2,1,0:T(8,128)}, f32[1,12,256]{2,1,0:T(8,128)}, s32[1]{0:T(128)}, s32[]{:T(128)}, /*index=5*/s32[16,1]{0,1:T(1,1...) while((s32[]{:T(128)}, f32[1,12,256,64]{3,2,1,0:T(8,128)}, ...), condition=%wide.region_8.9_spmd.clone, body=%wide.region_7.8_spmd.clone.sunk | while | flops 798738 | bytes 5640575 | solution.py:43
  305.4 174.7 %while.76 = (s32[]{:T(128)}, f32[1,12,256,64]{3,2,1,0:T(8,128)}, f32[1,12,256]{2,1,0:T(8,128)S(1)}, s32[1]{0:T(128)}, s32[]{:T(128)}, /*index=5*/s32[16,1]{0,1:T...) while((s32[]{:T(128)}, f32[1,12,256,64]{3,2,1,0:T(8,128)}, ...), condition=%wide.region_4.5_spmd.clone, body=%wide.region_3.4_spmd.clone.sunk | while | flops 798734 | bytes 5542153 | solution.py:43
  482.0 4.4 fusion.31
  486.4 3.7 fusion.26
  493.3 8.1 multiply_convert_fusion.2
  505.0 3.6 add_convert_fusion
  513.0 5.5 fusion.10
  519.4 5.8 fusion.172
  528.4 3.5 copy.120
  534.3 23.0 %all-gather.11 = f32[16,12,256]{2,1,0:T(8,128)} all-gather(f32[1,12,256]{2,1,0:T(8,128)S(1)} %bitcast.469), channel_id=9, replica_groups=mesh['dp'=2,'seq'=16] {'seq'}, dimensions={0}, use_global_device_ids=true | all-gather | bytes 208896 | tf_op jit(solution)/shard_map/all_gather | solution.py:30
  557.3 21.0 %all-gather.10 = f32[16,12,256]{2,1,0:T(8,128)} all-gather(f32[1,12,256]{2,1,0:T(8,128)S(1)} %bitcast.468), channel_id=7, replica_groups=mesh['dp'=2,'seq'=16] {'seq'}, dimensions={0}, use_global_device_ids=true | all-gather | bytes 208896 | tf_op jit(solution)/shard_map/all_gather | solution.py:30
  578.4 42.0 %all-gather.38.cloned.1.call-done = f32[192,256,64]{1,2,0:T(8,128)} async-done(((f32[12,256,64]{1,2,0:T(8,128)}), f32[192,256,64]{1,2,0:T(8,128)}) %all-gather.38.cloned.1.call-update) | async-done | bytes 12582928 | tf_op jit(solution)/shard_map/all_gather | solution.py:30
  620.4 175.1 %while.79 = (s32[]{:T(128)}, f32[1,12,256,64]{3,2,1,0:T(8,128)}, f32[1,12,256]{2,1,0:T(8,128)}, s32[1]{0:T(128)}, s32[]{:T(128)}, /*index=5*/s32[16,1]{0,1:T(1,1...) while((s32[]{:T(128)}, f32[1,12,256,64]{3,2,1,0:T(8,128)}, ...), condition=%wide.region_29.30_spmd.clone, body=%wide.region_28.29_spmd.clone.sunk | while | flops 798738 | bytes 5640575 | solution.py:43
  636.3 2.9 fusion.231
  647.3 2.9 fusion.231
  658.2 2.9 fusion.231
  669.5 2.9 fusion.231
  680.5 2.9 fusion.231
  691.5 2.9 fusion.231
  713.5 2.9 fusion.231
  724.5 2.9 fusion.231
  735.5 2.9 fusion.231
  757.7 2.9 fusion.231
  768.7 2.9 fusion.231
  779.8 2.9 fusion.231
  795.5 173.0 %while.78 = (s32[]{:T(128)}, f32[1,12,256,64]{3,2,1,0:T(8,128)}, f32[1,12,256]{2,1,0:T(8,128)S(1)}, s32[1]{0:T(128)}, s32[]{:T(128)}, /*index=5*/s32[16,1]{0,1:T...) while((s32[]{:T(128)}, f32[1,12,256,64]{3,2,1,0:T(8,128)}, ...), condition=%wide.region_25.26_spmd.clone, body=%wide.region_24.25_spmd.clone.sunk | while | flops 798734 | bytes 5542153 | solution.py:43
  974.4 4.2 fusion.32
  983.5 3.2 copy.122
  986.7 2.9 fusion.8
  992.3 3.2 copy.124
  997.7 6.8 fusion.156
  1006.3 6.1 fusion.116
  1014.4 34.1 %reduce-scatter.21.cloned.1.call-done = f32[48,768]{1,0:T(8,128)} async-done(((f32[768,768]{1,0:T(8,128)}), f32[48,768]{1,0:T(8,128)}) %reduce-scatter.21.cloned.1.call-update) | async-done | bytes 147472
  1050.3 64.8 %reduce-scatter.23.cloned.1.call-done = f32[48,768]{1,0:T(8,128)} async-done(((f32[768,768]{1,0:T(8,128)}), f32[48,768]{1,0:T(8,128)}) %reduce-scatter.23.cloned.1.call-update) | async-done | bytes 147472
  1116.9 64.8 %reduce-scatter.13.cloned.1.call-done = f32[48,768]{1,0:T(8,128)} async-done(((f32[768,768]{1,0:T(8,128)}), f32[48,768]{1,0:T(8,128)}) %reduce-scatter.13.cloned.1.call-update) | async-done | bytes 147472 | tf_op jit(solution)/shard_map/reduce_scatter | solution.py:308
  1181.7 114.9 %reduce-scatter.15.cloned.1.call-done = f32[48,3072]{1,0:T(8,128)} async-done(((f32[768,3072]{1,0:T(8,128)}), f32[48,3072]{1,0:T(8,128)}) %reduce-scatter.15.cloned.1.call-update) | async-done | bytes 589840 | tf_op jit(solution)/shard_map/reduce_scatter | solution.py:309
  1296.6 115.4 %reduce-scatter.17.cloned.1.call-done = f32[192,768]{1,0:T(8,128)} async-done(((f32[3072,768]{1,0:T(8,128)}), f32[192,768]{1,0:T(8,128)}) %reduce-scatter.17.cloned.1.call-update) | async-done | bytes 589840 | tf_op jit(solution)/shard_map/reduce_scatter | solution.py:310
  1412.1 74.8 %all-reduce.18.cloned.1.call-done = (f32[48,768]{0,1:T(8,128)}, f32[48,768]{0,1:T(8,128)}, f32[48,768]{0,1:T(8,128)}, f32[48,768]{1,0:T(8,128)}, f32[48,3072]{1,0:T(8,128)}, /*index=5*/f32[192,768]{1,0:T(8,128)}) async-done(((f32[48,768]{0,1:T(8,128)}, f32[48,768]{0,1:T(8,128)}, f32[48,768]{0,1:T(8,128)}, f32[48,768]{1,0:T(8,128)}, f32[48,3072]{1,0:T(8,128)}, /*index=5*/f32[192,768]{1,0:T(8,128)}), ...) | async-done | bytes 1769488 | tf_op jit(solution)/shard_map/psum | solution.py:316
  1493.8 4.4 collective-permute-start.1
  1498.3 10.1 collective-permute-done
  1513.7 8.3 collective-permute-done.2
  1522.0 7.3 collective-permute-start.4
  1529.3 10.4 collective-permute-done.4
  1539.7 5.4 collective-permute-start.6
  1547.5 7.6 collective-permute-done.6
  1555.2 6.0 collective-permute-start.8
  1562.6 60.8 %all-reduce.13 = (f32[768]{0:T(1024)S(1)}, f32[768]{0:T(1024)S(1)}, f32[768]{0:T(1024)S(1)}, f32[768]{0:T(1024)S(1)}) all-reduce(f32[768]{0:T(1024)S(1)} %copy-done.98, f32[768]{0:T(1024)S(1)} %copy-done.99, f32[768]{0:T(1024)S(1)} %copy-done.80, f32[768]{0:T(1024)S(1)} %convert_reduce_fusion), channel_id=16, replica_groups=mesh['dp'=2,'seq'=16] {'seq'}, use_global_device_ids=true, to_apply=%region_45.46.clone | all-reduce | flops 3072 | bytes 24576
  1623.7 4.9 all-reduce.14
  1629.4 58.3 %all-reduce.12 = (f32[768]{0:T(1024)}, f32[768]{0:T(1024)}, f32[768]{0:T(1024)}, f32[768]{0:T(1024)}) all-reduce(f32[768]{0:T(1024)S(1)} %dynamic-update-slice.3, f32[768]{0:T(1024)S(1)} %dynamic-update-slice.4, f32[768]{0:T(1024)S(1)} %dynamic-update-slice.5, f32[768]{0:T(1024)S(1)} %dynamic-update-slice.6), channel_id=1, replica_groups=mesh['dp'=2,'seq'=16] {'seq'}, use_global_device_ids=true, to_apply=%add.3 | all-reduce | flops 3072 | bytes 24576
  1692.7 4.3 broadcast_in_dim.440
  1700.5 3.6 collective-permute-done.9
  1704.1 4.5 collective-permute-start.11
  1710.6 5.6 collective-permute-done.10
  1723.9 4.4 collective-permute-start.13
  1733.8 14.4 collective-permute-done.13
  1749.2 6.1 collective-permute-done.14
  1757.2 23.5 %all-gather.30.cloned.1.call-done = f32[768,3072]{1,0:T(8,128)} async-done(((f32[48,3072]{1,0:T(8,128)}), f32[768,3072]{1,0:T(8,128)}) %all-gather.30.cloned.1.call-update) | async-done | bytes 9437200 | tf_op jit(solution)/shard_map/all_gather | solution.py:336
  1780.7 3.4 copy.286
  1790.4 3.7 copy.290
  (877 shorter events, 576.5 us)
Async XLA Ops:
  7.2 484.1 %copy-start = (bf16[768,768]{1,0:T(8,128)(2,1)S(1)}, bf16[768,768]{1,0:T(8,128)(2,1)}, u32[]{:S(2)}) copy-start(bf16[768,768]{1,0:T(8,128)(2,1)} %param.28) | copy-start | bytes 3538948
  7.2 122.6 %all-gather.34.cloned.1.call-start = ((), (), s32[]{:S(2)}) async-start(), calls=%async_computation.15 | async-start | bytes 13369344 | tf_op jit(solution)/shard_map/all_gather | solution.py:30
  9.4 8.0 copy-start.13
  15.0 8.0 copy-start.85
  15.0 8.0 copy-start.88
  17.5 7.6 copy-start.102
  23.0 26.7 %copy-start.18 = (bf16[1,256,12,256]{1,3,2,0:T(8,128)(2,1)S(1)}, bf16[1,256,12,256]{1,3,2,0:T(8,128)(2,1)}, u32[]{:S(2)}) copy-start(bf16[1,256,12,256]{1,3,2,0:T(8,128)(2,1)} %copy-done.17) | copy-start | bytes 4718596
  23.0 282.3 %all-gather.32.cloned.1.call-start = ((), (), s32[]{:S(2)}) async-start(), calls=%async_computation.14 | async-start | bytes 13369344 | tf_op jit(solution)/shard_map/all_gather | solution.py:30
  23.8 596.6 %all-gather.38.cloned.1.call-start = ((), (), s32[]{:S(2)}) async-start(), calls=%async_computation.17 | async-start | bytes 13369344 | tf_op jit(solution)/shard_map/all_gather | solution.py:30
  47.5 50.9 %copy-start.15 = (f32[256,768]{0,1:T(8,128)}, f32[256,768]{0,1:T(8,128)S(1)}, u32[]{:S(2)}) copy-start(f32[256,768]{0,1:T(8,128)S(1)} %copy.83) | copy-start | bytes 2359300
  49.7 46.3 %copy-start.23 = (bf16[12,64,256]{2,1,0:T(8,128)(2,1)S(1)}, bf16[12,64,256]{2,1,0:T(8,128)(2,1)}, u32[]{:S(2)}) copy-start(bf16[12,64,256]{2,1,0:T(8,128)(2,1)} %param.24) | copy-start | bytes 1179652
  49.7 46.3 %copy-start.43 = (bf16[256,768]{0,1:T(8,128)(2,1)S(1)}, bf16[256,768]{0,1:T(8,128)(2,1)}, u32[]{:S(2)}) copy-start(bf16[256,768]{0,1:T(8,128)(2,1)} %copy.82) | copy-start | bytes 1179652
  490.1 22.8 %copy-start.56 = (f32[256,12]{0,1:T(8,128)}, f32[256,12]{0,1:T(8,128)S(1)}, u32[]{:S(2)}) copy-start(f32[256,12]{0,1:T(8,128)S(1)} %get-tuple-element.1168) | copy-start | bytes 36868
  490.1 22.9 %copy-start.20 = (bf16[1,256,12,256]{1,3,2,0:T(8,128)(2,1)}, bf16[1,256,12,256]{1,3,2,0:T(8,128)(2,1)S(1)}, u32[]{:S(2)}) copy-start(bf16[1,256,12,256]{1,3,2,0:T(8,128)(2,1)S(1)} %get-tuple-element.1169) | copy-start | bytes 4718596
  491.6 9.8 slice-start
  492.1 19.0 %copy-start.8 = (f32[256,768]{1,0:T(8,128)}, f32[256,768]{1,0:T(8,128)S(1)}, u32[]{:S(2)}) copy-start(f32[256,768]{1,0:T(8,128)S(1)} %get-tuple-element.1191) | copy-start | bytes 2359300
  492.2 19.0 %copy-start.74 = (f32[256]{0:T(256)}, f32[256]{0:T(256)S(1)}, u32[]{:S(2)}) copy-start(f32[256]{0:T(256)S(1)} %broadcast_multiply_fusion.9) | copy-start | bytes 3076
  493.2 17.9 copy-start.81
  493.2 8.2 slice-start.1
  518.6 276.9 %all-gather.36.cloned.1.call-start = ((), (), s32[]{:S(2)}) async-start(), calls=%async_computation.16 | async-start | bytes 13369344 | tf_op jit(solution)/shard_map/all_gather | solution.py:30
  519.2 493.3 %reduce-scatter.19.cloned.1.call-start = ((), (), s32[]{:S(2)}) async-start(), calls=%async_computation.18 | async-start | bytes 2506752
  578.3 470.1 %reduce-scatter.21.cloned.1.call-start = ((), (), s32[]{:S(2)}) async-start(), calls=%async_computation.19 | async-start | bytes 2506752
  631.7 7.5 copy-start.44
  642.7 7.5 copy-start.44
  664.9 7.5 copy-start.44
  686.9 7.5 copy-start.44
  697.9 7.5 copy-start.44
  708.9 7.5 copy-start.44
  730.9 7.5 copy-start.44
  764.1 7.5 copy-start.44
  775.2 7.5 copy-start.44
  986.6 128.4 %reduce-scatter.23.cloned.1.call-start = ((), (), s32[]{:S(2)}) async-start(), calls=%async_computation.20 | async-start | bytes 2506752
  995.5 186.2 %reduce-scatter.13.cloned.1.call-start = ((), (), s32[]{:S(2)}) async-start(), calls=%async_computation.9 | async-start | bytes 2506752 | tf_op jit(solution)/shard_map/reduce_scatter | solution.py:308
  997.6 299.0 %reduce-scatter.15.cloned.1.call-start = ((), (), s32[]{:S(2)}) async-start(), calls=%async_computation.11 | async-start | bytes 10027008 | tf_op jit(solution)/shard_map/reduce_scatter | solution.py:309
  1004.6 407.4 %reduce-scatter.17.cloned.1.call-start = ((), (), s32[]{:S(2)}) async-start(), calls=%async_computation.13 | async-start | bytes 10027008 | tf_op jit(solution)/shard_map/reduce_scatter | solution.py:310
  1012.4 474.5 %all-reduce.18.cloned.1.call-start = ((), (), s32[]{:S(2)}) async-start(), calls=%async_computation.21 | async-start | bytes 5013504 | tf_op jit(solution)/shard_map/psum | solution.py:316
  1116.9 444.2 %copy-start.25 = (bf16[768,768]{1,0:T(8,128)(2,1)S(1)}, bf16[768,768]{1,0:T(8,128)(2,1)}, u32[]{:S(2)}) copy-start(bf16[768,768]{1,0:T(8,128)(2,1)} %param.25) | copy-start | bytes 3538948
  1116.9 444.2 %copy-start.28 = (bf16[1,256,12,64]{1,3,2,0:T(8,128)(2,1)S(1)}, bf16[1,256,12,64]{1,3,2,0:T(8,128)(2,1)}, u32[]{:S(2)}) copy-start(bf16[1,256,12,64]{1,3,2,0:T(8,128)(2,1)} %copy-done.27) | copy-start | bytes 1179652
  1412.1 337.1 %all-gather.22.cloned.1.call-start = ((), (), s32[]{:S(2)}) async-start(), calls=%async_computation.6 | async-start | bytes 2506752 | tf_op jit(solution)/shard_map/all_gather | solution.py:332
  1488.7 73.8 %copy-start.80 = (f32[768]{0:T(1024)S(1)}, f32[768]{0:T(1024)}, u32[]{:S(2)}) copy-start(f32[768]{0:T(1024)} %get-tuple-element.1056) | copy-start | bytes 9220
  1488.7 73.8 %copy-start.98 = (f32[768]{0:T(1024)S(1)}, f32[768]{0:T(1024)}, u32[]{:S(2)}) copy-start(f32[768]{0:T(1024)} %get-tuple-element.1054) | copy-start | bytes 9220
  1488.7 73.8 %copy-start.99 = (f32[768]{0:T(1024)S(1)}, f32[768]{0:T(1024)}, u32[]{:S(2)}) copy-start(f32[768]{0:T(1024)} %get-tuple-element.1059) | copy-start | bytes 9220
  1488.8 198.9 %copy-start.26 = (bf16[768,768]{1,0:T(8,128)(2,1)S(1)}, bf16[768,768]{1,0:T(8,128)(2,1)}, u32[]{:S(2)}) copy-start(bf16[768,768]{1,0:T(8,128)(2,1)} %param.26) | copy-start | bytes 3538948
  1488.8 260.4 %all-gather.24.cloned.1.call-start = ((), (), s32[]{:S(2)}) async-start(), calls=%async_computation.7 | async-start | bytes 2506752 | tf_op jit(solution)/shard_map/all_gather | solution.py:333
  1490.7 258.4 %all-gather.26.cloned.1.call-start = ((), (), s32[]{:S(2)}) async-start(), calls=%async_computation.8 | async-start | bytes 2506752 | tf_op jit(solution)/shard_map/all_gather | solution.py:334
  1492.6 256.5 %all-gather.28.cloned.1.call-start = ((), (), s32[]{:S(2)}) async-start(), calls=%async_computation.10 | async-start | bytes 2506752 | tf_op jit(solution)/shard_map/all_gather | solution.py:335
  1493.2 287.5 %all-gather.30.cloned.1.call-start = ((), (), s32[]{:S(2)}) async-start(), calls=%async_computation.12 | async-start | bytes 10027008 | tf_op jit(solution)/shard_map/all_gather | solution.py:336
  1493.8 14.6 collective-permute-start
  1493.8 17.4 collective-permute-start.1
  1509.2 12.8 collective-permute-start.2
  1511.3 10.7 copy-start.52
  1511.3 18.0 collective-permute-start.3
  1522.0 17.7 collective-permute-start.4
  1529.3 18.2 %collective-permute-start.5 = (f32[192,768]{1,0:T(8,128)}, f32[192,768]{1,0:T(8,128)}, u32[]{:S(2)}, u32[]{:S(2)}) collective-permute-start(f32[192,768]{1,0:T(8,128)} %collective-permute-done.3), channel_id=1, source_target_pairs={{0,15},{1,0},{2,1},{3,2},{4,3},{5,4},{6,5},{7,6},{8,7},{9,8},{10,9... | collective-permute-start | bytes 1769480 | tf_op jit(solution)/shard_map/ppermute | solution.py:21
  1539.7 15.5 collective-permute-start.6
  1547.5 141.9 %collective-permute-start.7 = (f32[192,768]{1,0:T(8,128)}, f32[192,768]{1,0:T(8,128)}, u32[]{:S(2)}, u32[]{:S(2)}) collective-permute-start(f32[192,768]{1,0:T(8,128)} %collective-permute-done.5), channel_id=1, source_target_pairs={{0,15},{1,0},{2,1},{3,2},{4,3},{5,4},{6,5},{7,6},{8,7},{9,8},{10,9... | collective-permute-start | bytes 1769480 | tf_op jit(solution)/shard_map/ppermute | solution.py:21
  1555.2 137.0 %collective-permute-start.8 = (f32[192,768]{1,0:T(8,128)}, f32[192,768]{1,0:T(8,128)}, u32[]{:S(2)}, u32[]{:S(2)}) collective-permute-start(f32[192,768]{1,0:T(8,128)} %collective-permute-done.6), channel_id=1, source_target_pairs={{0,1},{1,2},{2,3},{3,4},{4,5},{5,6},{6,7},{7,8},{8,9},{9,10},{10,1... | collective-permute-start | bytes 1769480 | tf_op jit(solution)/shard_map/ppermute | solution.py:18
  1689.4 14.7 collective-permute-start.9
  1692.2 24.0 %collective-permute-start.10 = (f32[192,768]{1,0:T(8,128)}, f32[192,768]{1,0:T(8,128)S(1)}, u32[]{:S(2)}, u32[]{:S(2)}) collective-permute-start(f32[192,768]{1,0:T(8,128)} %collective-permute-done.8), channel_id=1, source_target_pairs={{0,1},{1,2},{2,3},{3,4},{4,5},{5,6},{6,7},{7,8},{8,9},{9,10},{10,1... | collective-permute-start | bytes 1769480 | tf_op jit(solution)/shard_map/ppermute | solution.py:18
  1704.1 19.7 %collective-permute-start.11 = (f32[192,768]{1,0:T(8,128)S(1)}, f32[192,768]{1,0:T(8,128)S(1)}, u32[]{:S(2)}, u32[]{:S(2)}) collective-permute-start(f32[192,768]{1,0:T(8,128)S(1)} %collective-permute-done.9), channel_id=1, source_target_pairs={{0,15},{1,0},{2,1},{3,2},{4,3},{5,4},{6,5},{7,6},{8,7},{9,8},{10,9... | collective-permute-start | bytes 1769480 | tf_op jit(solution)/shard_map/ppermute | solution.py:21
  1716.2 14.2 collective-permute-start.12
  1723.9 24.4 %collective-permute-start.13 = (f32[192,768]{1,0:T(8,128)S(1)}, f32[192,768]{1,0:T(8,128)S(1)}, u32[]{:S(2)}, u32[]{:S(2)}) collective-permute-start(f32[192,768]{1,0:T(8,128)S(1)} %collective-permute-done.11), channel_id=1, source_target_pairs={{0,15},{1,0},{2,1},{3,2},{4,3},{5,4},{6,5},{7,6},{8,7},{9,8},{10,9... | collective-permute-start | bytes 1769480 | tf_op jit(solution)/shard_map/ppermute | solution.py:21
  1730.4 24.9 %collective-permute-start.14 = (f32[192,768]{1,0:T(8,128)S(1)}, f32[192,768]{1,0:T(8,128)}, u32[]{:S(2)}, u32[]{:S(2)}) collective-permute-start(f32[192,768]{1,0:T(8,128)S(1)} %collective-permute-done.12), channel_id=1, source_target_pairs={{0,1},{1,2},{2,3},{3,4},{4,5},{5,6},{6,7},{7,8},{8,9},{9,10},{10,1... | collective-permute-start | bytes 1769480 | tf_op jit(solution)/shard_map/ppermute | solution.py:18
  1749.1 35.0 %copy-start.38 = (f32[768,768]{1,0:T(8,128)S(1)}, f32[768,768]{1,0:T(8,128)}, u32[]{:S(2)}) copy-start(f32[768,768]{1,0:T(8,128)} %all-gather.24.cloned.1.call-done) | copy-start | bytes 7077892
  (134 other events, 470.7 us)
Sparse Core Ops, SparseCore 0:
  23.1 106.6 all-gather.33
  132.6 98.6 all-gather.31
  518.7 101.6 all-gather.37
  622.5 99.2 all-gather.35
  726.0 61.4 reduce-scatter.18
  986.8 61.6 reduce-scatter.20
  1052.8 62.2 reduce-scatter.22
  1119.4 62.2 reduce-scatter.12
  1186.4 110.2 reduce-scatter.14
  1301.1 110.8 reduce-scatter.16
  1415.3 71.6 all-reduce.17
  1489.6 59.3 all-gather.21
  1551.3 45.4 all-gather.23
  1599.0 41.2 all-gather.25
  1642.4 41.7 all-gather.27
  1686.3 94.3 all-gather.29
